TPU v7x, 128 devices: a whole 4x4x4 slice. The times are simulated.
128 devices in a mesh: exp: 32 (over z, x_lo, y), row: 4 (over x_hi, core).
Axes of the slice: x: 4 (x_hi: 2, x_lo: 2; x = x_hi * 2 + x_lo), y: 4, z: 4, core: 2. Of those that a mesh axis runs over, the one named last changes fastest.
Arguments:
- latent: bfloat16 [4, 1024, 1024], P(None, 'row', 'exp'), may hold values from -6 to 6
- row_taps: bfloat16 [16, 21], replicated, may hold values from -1.25 to 1.25
- column_taps: bfloat16 [16, 21], replicated, may hold values from -1.25 to 1.25
- coefficients: bfloat16 [32, 16, 1024, 1024], P('exp', None, 'row'), may hold values from -1.5 to 1.5
- observed: bfloat16 [32, 1024, 1024], P('exp', 'row'), may hold values from -6 to 6
- cell_of: int32 [32, 1], replicated, may hold values from 0 to 3
- valid_rows: int32 [32, 1024], P('exp', 'row'), may hold values 0 or 1
Outputs:
- gradient: float32 [4, 1024, 1024], P(None, 'row', 'exp')
- residuals: float32 [32, 1024, 1024], P('exp', 'row')
Inputs may be any that keep to these rules, and one draw needn't show every extreme that they name: `cell_of`: every sky cell is covered by at least one exposure.
All inputs are finite; a program needn't handle non-finite values. No bound on the sum of `valid_rows` on one device may be relied on, other than what follows from the above.
Results may differ from a plain program's by a relative error of at most 0.0023.
Values may be sent and summed in bfloat16 or wider, within the bound.
No kernel may reach another device: no remote copies, remote signals or barrier semaphores. Data moves between devices by JAX's collectives and lax.ppermute only.
A program may use at most 128 MiB of HBM per device.

v0:
```python
import jax
import jax.numpy as jnp
from jax import lax
from jax.sharding import PartitionSpec as P


def padded_2(cells, sides, width):
    for axis, dim in sides:
        count = lax.axis_size(axis)
        ends = count - 1
        head = lax.slice_in_dim(cells, 0, width, axis=dim)
        tail = lax.slice_in_dim(cells, cells.shape[dim] - width, cells.shape[dim], axis=dim)
        cells = jnp.concatenate(
            [
                lax.ppermute(tail, axis, [(i, (i + 1) % count) for i in range(ends)]),
                cells,
                lax.ppermute(head, axis, [((i + 1) % count, i) for i in range(ends)]),
            ],
            axis=dim,
        )
    return cells


def from_behind(block, axis, distance):
    devices = range(lax.axis_size(axis))
    route = [(i - distance, i) for i in devices if i - distance in devices]
    return lax.ppermute(block, axis, route)


def bands(kernel_taps, adjoint):
    tap_count = kernel_taps.shape[1]
    halfwidth = tap_count // 2
    inputs_at = lax.broadcasted_iota(jnp.int32, (384, 128), 0)
    outputs_at = lax.broadcasted_iota(jnp.int32, (384, 128), 1)
    if adjoint:
        offset = outputs_at - inputs_at + 128 + halfwidth
    else:
        offset = inputs_at - 128 - outputs_at + halfwidth
    onehot = (offset[:, :, None] == jnp.arange(tap_count)[None, None, :]).astype(jnp.float32)
    return jnp.einsum("kt,pqt->kpq", kernel_taps.astype(jnp.float32), onehot).astype(jnp.bfloat16)


def column_matrix(kernel_taps, strip_rows):
    tap_count = kernel_taps.shape[1]
    halfwidth = tap_count // 2
    outputs_at = lax.broadcasted_iota(jnp.int32, (strip_rows, strip_rows + 2 * halfwidth), 0)
    inputs_at = lax.broadcasted_iota(jnp.int32, (strip_rows, strip_rows + 2 * halfwidth), 1)
    offset = inputs_at - outputs_at
    onehot = (offset[:, :, None] == jnp.arange(tap_count)[None, None, :]).astype(jnp.float32)
    return jnp.einsum("kt,yit->kyi", kernel_taps.astype(jnp.float32), onehot).astype(jnp.bfloat16)


def stacked_blocks(source):
    length = source.shape[-1]
    nblocks = length // 128
    padding = [(0, 0)] * (source.ndim - 1) + [(128, 128)]
    padded = jnp.pad(source, padding)
    blocked = padded.reshape(source.shape[:-1] + (nblocks + 2, 128))
    return jnp.concatenate(
        [blocked[..., :-2, :], blocked[..., 1:-1, :], blocked[..., 2:, :]], axis=-1
    )


def body(latent, row_taps, column_taps, coefficients, observed, cell_of, valid_rows):
    tap_count = row_taps.shape[1]
    halfwidth = tap_count // 2
    kernel_count = row_taps.shape[0]
    strip_rows = observed.shape[1]
    cell_width = observed.shape[2]
    ncells = latent.shape[0]
    position = lax.axis_index("exp")
    cell_list = cell_of[:, 0]
    own_cell = lax.dynamic_index_in_dim(cell_list, position, 0, keepdims=False)
    all_cells = lax.all_gather(latent, "exp", axis=2, tiled=True)
    cell_strip = lax.dynamic_index_in_dim(all_cells, own_cell, 0, keepdims=False)
    extended = padded_2(cell_strip, (("row", 0),), halfwidth)
    rowblur = jnp.einsum(
        "rbp,kpq->krbq",
        stacked_blocks(extended),
        bands(row_taps, False),
        preferred_element_type=jnp.float32,
    )
    rowblur = rowblur.reshape(kernel_count, strip_rows + 2 * halfwidth, cell_width).astype(
        jnp.bfloat16
    )
    matrix = column_matrix(column_taps, strip_rows)
    vertical = jnp.einsum("kyi,kix->kyx", matrix, rowblur, preferred_element_type=jnp.float32)
    coeffs = coefficients[0].astype(jnp.float32)
    predicted = jnp.sum(coeffs * vertical, axis=0)
    row_mask = valid_rows[0].astype(jnp.float32)[:, None]
    residual = row_mask * (predicted - observed[0].astype(jnp.float32))
    weighted = (coeffs * residual[None]).astype(jnp.bfloat16)
    colback_ext = jnp.einsum("kyi,kyx->kix", matrix, weighted, preferred_element_type=jnp.float32)
    upper_rim = colback_ext[:, :halfwidth]
    lower_rim = colback_ext[:, strip_rows + halfwidth :]
    from_below = from_behind(upper_rim.astype(jnp.bfloat16), "row", -1).astype(upper_rim.dtype)
    from_above = from_behind(lower_rim.astype(jnp.bfloat16), "row", 1).astype(lower_rim.dtype)
    middle = colback_ext[:, halfwidth : strip_rows + halfwidth]
    middle = middle.at[:, :halfwidth].add(from_above)
    middle = middle.at[:, strip_rows - halfwidth :].add(from_below)
    colback = middle.astype(jnp.bfloat16)
    own_term = jnp.einsum(
        "krbp,kpq->rbq",
        stacked_blocks(colback),
        bands(row_taps, True),
        preferred_element_type=jnp.float32,
    ).reshape(strip_rows, cell_width)
    selector = (jnp.arange(ncells) == own_cell).astype(jnp.float32)
    gradient = lax.psum_scatter(
        selector[:, None, None] * own_term[None], "exp", scatter_dimension=2, tiled=True
    )
    return (gradient, residual[None])


def solution(mesh):
    placed = (
        P(None, "row", "exp"),
        P(),
        P(),
        P("exp", None, "row", None),
        P("exp", "row", None),
        P(),
        P("exp", "row"),
    )
    return jax.shard_map(
        body,
        mesh=mesh,
        in_specs=placed,
        out_specs=(P(None, "row", "exp"), P("exp", "row", None)),
        check_vma=False,
    )
```

profile of v0, /device:TPU:4, one launch (start us, length us, event | category | flops | bytes accessed | tf_op | source)
XLA Modules:
  0.0 556.6 jit_solution(14296747167301705185)
XLA Ops:
  7.2 1.5 copy.41
  11.9 2.3 fusion.28
  14.2 2.2 convert_bitcast_fusion.1
  16.4 148.6 %all-gather.2.cloned.1.call-done = bf16[4,256,1024]{1,0,2:T(4,128)(2,1)} async-done(((bf16[4,256,32]{1,0,2:T(4,128)(2,1)}), bf16[4,256,1024]{1,0,2:T(4,128)(2,1)}) %all-gather.2.cloned.1.call-update) | async-done | bytes 2097168 | tf_op jit(solution)/shard_map/all_gather | solution.py:74
  165.0 2.7 constant_dynamic-slice_fusion
  167.7 2.3 copy.62
  170.7 1.9 collective-permute-start
  172.7 5.3 collective-permute-start.1
  179.4 2.0 fusion.36
  184.4 7.2 %convert_bitcast_fusion = bf16[16,276,8,128]{3,1,2,0:T(8,128)(2,1)} fusion(bf16[276,8,128]{2,0,1:T(8,128)(2,1)S(1)} %copy.65, bf16[276,8,128]{2,0,1:T(8,128)(2,1)S(1)} %copy.64, bf16[276,8,128]{2,0,1:T(8,128)(2,1)S(1)} %copy.63, bf16[16,384,128,1]{2,0,1,3:T(8,128)(2,1)S(1)} %copy-done.3), kind=kOutput, calls=%fused_computation.10 | convolution fusion | flops 3482492928 | bytes 12312576 | tf_op jit(solution)/shard_map/rbp,kpq->krbq/dot_general | solution.py:77
  191.6 8.3 %copy.60 = bf16[16,276,8,128]{3,2,1,0:T(8,128)(2,1)} copy(bf16[16,276,8,128]{3,1,2,0:T(8,128)(2,1)} %convert_bitcast_fusion) | data formatting | bytes 18087936 | tf_op jit(solution)/shard_map/convert_element_type | solution.py:83
  199.9 14.0 %reshape.143 = bf16[16,276,1024]{2,1,0:T(8,128)(2,1)} reshape(bf16[16,276,8,128]{3,2,1,0:T(8,128)(2,1)} %copy.60) | data formatting | bytes 18087936 | tf_op jit(solution)/shard_map/convert_element_type | solution.py:83
  213.8 13.0 %fusion.6 = f32[256,1024]{1,0:T(8,128)S(1)} fusion(bf16[16,276,1024]{2,1,0:T(8,128)(2,1)} %reshape.143, bf16[1,16,256,1024]{3,2,1,0:T(8,128)(2,1)} %param.14, bf16[16,256,276]{1,0,2:T(8,128)(2,1)S(1)} %convert_bitcast_fusion.1), kind=kOutput, calls=%fused_computation.8 | convolution fusion | flops 2327576576 | bytes 20742144 | tf_op jit(solution)/shard_map/kyi,kix->kyx/dot_general | solution.py:87
  227.0 17.7 %fusion.45 = (bf16[16,276,1024]{2,1,0:T(8,128)(2,1)}, f32[16,276,1024]{2,1,0:T(8,128)}) fusion(bf16[1,16,256,1024]{3,2,1,0:T(8,128)(2,1)} %param.14, f32[256,1024]{1,0:T(8,128)S(1)} %bitcast.54, bf16[16,256,276]{1,0,2:T(8,128)(2,1)S(1)} %convert_bitcast_fusion.1), kind=kOutput, calls=%fused_computation.67 | convolution fusion | flops 2332360704 | bytes 38830080 | tf_op jit(solution)/shard_map/kyi,kyx->kix/dot_general | solution.py:93
  244.7 2.4 fusion.43
  247.1 1.9 collective-permute-start.2
  250.1 5.2 collective-permute-start.3
  257.1 12.6 %slice.110 = f32[16,256,1024]{2,1,0:T(8,128)} slice(f32[16,276,1024]{2,1,0:T(8,128)} %get-tuple-element.37), slice={[0:16], [10:266], [0:1024]} | slice | bytes 33554432 | tf_op jit(solution)/shard_map/slice | solution.py:98
  269.7 1.7 slice_add_fusion.1
  271.4 5.8 %scatter-add.6 = f32[16,256,1024]{2,1,0:T(8,128)} dynamic-update-slice(f32[16,256,1024]{2,1,0:T(8,128)} %slice.110, f32[16,10,1024]{2,1,0:T(8,128)S(1)} %slice_add_fusion.1, s32[]{:T(128)} %constant.75.clone.1, s32[]{:T(128)} %constant.75.clone.1, s32[]{:T(128)} %constant.75.clone.1) | dynamic-update-slice | bytes 1310724 | tf_op jit(solution)/shard_map/scatter-add | solution.py:99
  277.3 1.5 slice_add_fusion
  278.8 5.1 scatter-add.9
  283.9 9.1 %convert_element_type.94 = bf16[16,256,1024]{2,1,0:T(8,128)(2,1)} convert(f32[16,256,1024]{2,1,0:T(8,128)} %scatter-add.9) | non-fusion elementwise | flops 4194304 | bytes 25165824 | tf_op jit(solution)/shard_map/convert_element_type | solution.py:101
  293.0 12.3 %copy.69 = bf16[16,256,1024]{1,2,0:T(8,128)(2,1)} copy(bf16[16,256,1024]{2,1,0:T(8,128)(2,1)} %convert_element_type.94) | data formatting | bytes 16777216
  305.3 8.4 %pad.13.clone = bf16[16,256,1280]{1,2,0:T(8,128)(2,1)} pad(bf16[16,256,1024]{1,2,0:T(8,128)(2,1)} %copy.69, bf16[]{:T(256)} %constant.80.clone.1), padding=0_0x0_0x128_128 | pad | bytes 18874370 | tf_op jit(solution)/shard_map/jit(_pad)/pad | solution.py:57
  313.7 16.7 %fusion.42 = (bf16[16,256,8,128]{1,3,2,0:T(8,128)(2,1)}, bf16[16,256,8,128]{1,3,2,0:T(8,128)(2,1)}, bf16[16,256,8,128]{1,3,2,0:T(8,128)(2,1)}) fusion(bf16[16,256,10,128]{1,3,2,0:T(8,128)(2,1)} %bitcast.53), kind=kLoop, calls=%fused_computation.64 | loop fusion | bytes 50331648 | tf_op jit(solution)/shard_map/slice | solution.py:60
  330.4 11.4 %copy.66 = bf16[16,256,8,128]{3,1,0,2:T(8,128)(2,1)} copy(bf16[16,256,8,128]{1,3,2,0:T(8,128)(2,1)} %get-tuple-element.26) | data formatting | bytes 16777216
  341.8 11.4 %copy.67 = bf16[16,256,8,128]{3,1,0,2:T(8,128)(2,1)} copy(bf16[16,256,8,128]{1,3,2,0:T(8,128)(2,1)} %get-tuple-element.27) | data formatting | bytes 16777216
  353.2 11.4 %copy.68 = bf16[16,256,8,128]{3,1,0,2:T(8,128)(2,1)} copy(bf16[16,256,8,128]{1,3,2,0:T(8,128)(2,1)} %get-tuple-element.28) | data formatting | bytes 16777216
  364.6 12.3 %fusion = f32[256,8,128,1]{0,2,3,1:T(8,128)S(1)} fusion(bf16[16,256,8,128]{3,1,0,2:T(8,128)(2,1)} %copy.68, bf16[16,256,8,128]{3,1,0,2:T(8,128)(2,1)} %copy.67, bf16[16,256,8,128]{3,1,0,2:T(8,128)(2,1)} %copy.66, bf16[16,384,128]{1,2,0:T(8,128)(2,1)S(1)} %copy.55), kind=kOutput, calls=%fused_computation | convolution fusion | flops 3296722944 | bytes 27787264 | tf_op jit(solution)/shard_map/krbp,kpq->rbq/dot_general | solution.py:102
  376.9 2.4 broadcast_multiply_fusion
  379.3 170.4 %reduce-scatter.2.cloned.1.call-done = f32[4,256,32]{1,2,0:T(8,128)} async-done(((f32[4,256,1024]{1,2,0:T(8,128)}), f32[4,256,32]{1,2,0:T(8,128)}) %reduce-scatter.2.cloned.1.call-update) | async-done | bytes 131088 | tf_op jit(solution)/shard_map/reduce_scatter | solution.py:109
  (38 shorter events, 9.7 us)
Async XLA Ops:
  7.2 4.7 copy-start
  7.2 171.5 %copy-start.6 = (s32[1,256]{1,0:T(1,128)S(1)}, s32[1,256]{1,0:T(1,128)}, u32[]{:S(2)}) copy-start(s32[1,256]{1,0:T(1,128)} %param.17) | copy-start | bytes 3076
  7.2 157.8 %all-gather.2.cloned.1.call-start = ((), (), s32[]{:S(2)}) async-start(), calls=%async_computation.1 | async-start | bytes 2162688 | tf_op jit(solution)/shard_map/all_gather | solution.py:74
  8.8 541.0 %reduce-scatter.2.cloned.1.call-start = ((), (), s32[]{:S(2)}) async-start(), calls=%async_computation.2 | async-start | bytes 4325376 | tf_op jit(solution)/shard_map/reduce_scatter | solution.py:109
  170.7 8.0 %collective-permute-start = (bf16[10,1024]{1,0:T(8,128)(2,1)S(1)}, bf16[10,1024]{1,0:T(8,128)(2,1)S(1)}, u32[]{:S(2)}, u32[]{:S(2)}) collective-permute-start(bf16[10,1024]{1,0:T(8,128)(2,1)S(1)} %get-tuple-element.34), channel_id=1, source_target_pairs={{0,1},{1,2},{2,3},{4,5},{5,6},{6,7},{8,9},{9,10},{10,11},{12,13},{... | collective-permute-start | bytes 61448 | tf_op jit(solution)/shard_map/ppermute | solution.py:15
  172.7 6.7 %collective-permute-start.1 = (bf16[10,1024]{1,0:T(8,128)(2,1)S(1)}, bf16[10,1024]{1,0:T(8,128)(2,1)S(1)}, u32[]{:S(2)}, u32[]{:S(2)}) collective-permute-start(bf16[10,1024]{1,0:T(8,128)(2,1)S(1)} %get-tuple-element.35), channel_id=1, source_target_pairs={{1,0},{2,1},{3,2},{5,4},{6,5},{7,6},{9,8},{10,9},{11,10},{13,12},{... | collective-permute-start | bytes 61448 | tf_op jit(solution)/shard_map/ppermute | solution.py:17
  182.9 1.4 copy-start.3
  213.8 13.0 %copy-start.5 = (bf16[1,256,1024]{2,1,0:T(8,128)(2,1)S(1)}, bf16[1,256,1024]{2,1,0:T(8,128)(2,1)}, u32[]{:S(2)}) copy-start(bf16[1,256,1024]{2,1,0:T(8,128)(2,1)} %param.15) | copy-start | bytes 1572868
  227.0 17.7 %copy-start.2 = (f32[1,256,1024]{2,1,0:T(8,128)}, f32[1,256,1024]{2,1,0:T(8,128)S(1)}, u32[]{:S(2)}) copy-start(f32[1,256,1024]{2,1,0:T(8,128)S(1)} %fusion.31) | copy-start | bytes 3145732
  227.0 22.0 %copy-start.4 = (s32[384,128]{1,0:T(8,128)S(1)}, s32[384,128]{1,0:T(8,128)}, u32[]{:S(2)}) copy-start(s32[384,128]{1,0:T(8,128)} %subtract_add_fusion) | copy-start | bytes 589828
  247.1 22.6 %collective-permute-start.2 = (bf16[16,10,1024]{2,1,0:T(8,128)(2,1)}, bf16[16,10,1024]{2,1,0:T(8,128)(2,1)}, u32[]{:S(2)}, u32[]{:S(2)}) collective-permute-start(bf16[16,10,1024]{2,1,0:T(8,128)(2,1)} %get-tuple-element.30), channel_id=1, source_target_pairs={{0,1},{1,2},{2,3},{4,5},{5,6},{6,7},{8,9},{9,10},{10,11},{12,13},{... | collective-permute-start | bytes 983048 | tf_op jit(solution)/shard_map/ppermute | solution.py:27
  250.1 27.1 %collective-permute-start.3 = (bf16[16,10,1024]{2,1,0:T(8,128)(2,1)}, bf16[16,10,1024]{2,1,0:T(8,128)(2,1)}, u32[]{:S(2)}, u32[]{:S(2)}) collective-permute-start(bf16[16,10,1024]{2,1,0:T(8,128)(2,1)} %get-tuple-element.29), channel_id=1, source_target_pairs={{1,0},{2,1},{3,2},{5,4},{6,5},{7,6},{9,8},{10,9},{11,10},{13,12},{... | collective-permute-start | bytes 983048 | tf_op jit(solution)/shard_map/ppermute | solution.py:27
  376.9 172.8 %copy-start.1 = (bf16[16,21]{1,0:T(8,128)(2,1)S(1)}, bf16[16,21]{1,0:T(8,128)(2,1)}, u32[]{:S(2)}) copy-start(bf16[16,21]{1,0:T(8,128)(2,1)} %param.12) | copy-start | bytes 2020
Sparse Core Ops, SparseCore 0:
  10.2 154.7 all-gather.1
  379.4 170.2 reduce-scatter.1
where the time goes:
time: 559 us; the launch traced here: 557 us
  waiting for transfers between devices  320 us (57%)
  local copies, waits for them, and re-layouts  132 us (24%)
  matrix products  55.8 us (10%)
  other arithmetic  18.3 us (3%)
  between operations  15.9 us (3%)
  starting transfers between devices  14.4 us (3%)
    reduce_scatter x1, waiting for transfers between devices, body(): lax.psum_scatter(selector[:, None, None] * own_term[None], 'exp', scatter...  170 us
    all_gather x1, waiting for transfers between devices, body(): all_cells = lax.all_gather(latent, 'exp', axis=2, tiled=True)  149 us
    unnamed x23, local copies, waits for them, and re-layouts  51.4 us
    convert_element_type x2, local copies, waits for them, and re-layouts, body(): rowblur.reshape(kernel_count, strip_rows + 2 * halfwidth, cell_width)  22.3 us
    dot_general x1, matrix products, body(): jnp.einsum('kyi,kyx->kix', matrix, weighted, preferred_element_type=jnp.f...  17.7 us
    slice x2, local copies, waits for them, and re-layouts, stacked_blocks(): blocked[..., :-2, :]  17 us
    dot_general x1, matrix products, body(): jnp.einsum('kyi,kix->kyx', matrix, rowblur, preferred_element_type=jnp.fl...  13 us
    slice x1, local copies, waits for them, and re-layouts, body(): middle = colback_ext[:, halfwidth:strip_rows + halfwidth]  12.6 us
  transfers between devices with their start and end apart: 6, of which 3 were waited for; matrix products, arithmetic and copies ran while one was open for 5% of the time, Pallas kernels for 0%

commit v1 on v0

--- a/solution.py
+++ b/solution.py
@@ -2,6 +2,13 @@
 import jax.numpy as jnp
 from jax import lax
 from jax.sharding import PartitionSpec as P
+
+
+def swapped_in(x, axis, along):
+    n_dev = lax.axis_size(axis)
+    tiles = jnp.stack([x for _ in range(n_dev)])
+    tiles = lax.all_to_all(tiles, axis, split_axis=0, concat_axis=0)
+    return jnp.concatenate(tiles, axis=along)
 
 
 def padded_2(cells, sides, width):
@@ -71,7 +78,7 @@
     position = lax.axis_index("exp")
     cell_list = cell_of[:, 0]
     own_cell = lax.dynamic_index_in_dim(cell_list, position, 0, keepdims=False)
-    all_cells = lax.all_gather(latent, "exp", axis=2, tiled=True)
+    all_cells = swapped_in(latent, "exp", 2)
     cell_strip = lax.dynamic_index_in_dim(all_cells, own_cell, 0, keepdims=False)
     extended = padded_2(cell_strip, (("row", 0),), halfwidth)
     rowblur = jnp.einsum(

time: 559 us -> 441 us (0.79)
  waiting for transfers between devices: 320 us -> 195 us
  starting transfers between devices: 14.4 us -> 23.6 us
    all_gather x1 -> x0, waiting for transfers between devices: 149 us -> none  [body(): all_cells = lax.all_gather(latent, 'exp', axis=2, tiled=True)]
    all_to_all x0 -> x1, waiting for transfers between devices: none -> 22.6 us  [swapped_in(): tiles = lax.all_to_all(tiles, axis, split_axis=0, concat_axis=0)]
    all_to_all x0 -> x1, starting transfers between devices: none -> 9.1 us  [swapped_in(): tiles = lax.all_to_all(tiles, axis, split_axis=0, concat_axis=0)]
    unnamed x23 -> x25, local copies, waits for them, and re-layouts: 51.4 us -> 47.6 us
  transfers between devices with their start and end apart: 6 -> 6, of which waited for: 3 -> 4; matrix products, arithmetic and copies ran while one was open for 5% -> 7% of each run, Pallas kernels for 0% -> 0%
where the time goes in v1:
time: 441 us; the launch traced here: 439 us
  waiting for transfers between devices  195 us (44%)
  local copies, waits for them, and re-layouts  132 us (30%)
  matrix products  55.2 us (13%)
  starting transfers between devices  23.6 us (5%)
  other arithmetic  17.4 us (4%)
  between operations  16.3 us (4%)
    reduce_scatter x1, waiting for transfers between devices, body(): lax.psum_scatter(selector[:, None, None] * own_term[None], 'exp', scatter...  169 us
    unnamed x25, local copies, waits for them, and re-layouts  47.6 us
    all_to_all x1, waiting for transfers between devices, swapped_in(): tiles = lax.all_to_all(tiles, axis, split_axis=0, concat_axis=0)  22.6 us
    convert_element_type x2, local copies, waits for them, and re-layouts, body(): rowblur.reshape(kernel_count, strip_rows + 2 * halfwidth, cell_width)  22.3 us
    dot_general x1, matrix products, body(): jnp.einsum('kyi,kyx->kix', matrix, weighted, preferred_element_type=jnp.f...  17.7 us
    slice x2, local copies, waits for them, and re-layouts, stacked_blocks(): blocked[..., :-2, :]  17 us
    dot_general x1, matrix products, body(): jnp.einsum('kyi,kix->kyx', matrix, rowblur, preferred_element_type=jnp.fl...  13 us
    slice x1, local copies, waits for them, and re-layouts, body(): middle = colback_ext[:, halfwidth:strip_rows + halfwidth]  12.6 us
  transfers between devices with their start and end apart: 6, of which 4 were waited for; matrix products, arithmetic and copies ran while one was open for 7% of the time, Pallas kernels for 0%

profile of v1, /device:TPU:4, one launch (start us, length us, event | category | flops | bytes accessed | tf_op | source)
XLA Modules:
  0.0 438.9 jit_solution(11858010761935252944)
XLA Ops:
  7.2 2.4 stack.2
  9.6 9.1 %all-to-all-start = ((bf16[32,4,256,32]{2,3,1,0:T(8,128)(2,1)}), bf16[32,4,256,32]{2,3,1,0:T(8,128)(2,1)}, u32[]{:S(2)}, u32[]{:S(2)}) async-start(bf16[32,4,256,32]{2,3,1,0:T(8,128)(2,1)} %stack.2), calls=%async_computation | async-start | bytes 4194304 | tf_op jit(solution)/shard_map/all_to_all | solution.py:10
  22.3 2.3 fusion.28
  24.6 1.5 convert_bitcast_fusion.1
  26.1 22.6 %all-to-all-done = bf16[32,4,256,32]{2,3,1,0:T(8,128)(2,1)} async-done(((bf16[32,4,256,32]{2,3,1,0:T(8,128)(2,1)}), bf16[32,4,256,32]{2,3,1,0:T(8,128)(2,1)}, u32[]{:S(2)}, u32[]{:S(2)}) %all-to-all-start) | async-done | bytes 2097184 | tf_op jit(solution)/shard_map/all_to_all | solution.py:10
  48.7 1.8 copy.44
  51.3 1.9 collective-permute-start
  53.2 5.3 %collective-permute-start.1 = (bf16[10,1024]{0,1:T(8,128)(2,1)}, bf16[10,1024]{0,1:T(8,128)(2,1)}, u32[]{:S(2)}, u32[]{:S(2)}) collective-permute-start(bf16[10,1024]{0,1:T(8,128)(2,1)} %get-tuple-element.32), channel_id=1, source_target_pairs={{1,0},{2,1},{3,2},{5,4},{6,5},{7,6},{9,8},{10,9},{11,10},{13,12},{... | collective-permute-start | bytes 61448 | tf_op jit(solution)/shard_map/ppermute | solution.py:24
  58.8 2.0 collective-permute-done
  67.6 7.2 %convert_bitcast_fusion = bf16[16,276,8,128]{3,1,2,0:T(8,128)(2,1)} fusion(bf16[276,8,128]{2,0,1:T(8,128)(2,1)S(1)} %copy.69, bf16[276,8,128]{2,0,1:T(8,128)(2,1)S(1)} %copy.68, bf16[276,8,128]{2,0,1:T(8,128)(2,1)S(1)} %copy.67, bf16[16,384,128,1]{2,0,1,3:T(8,128)(2,1)S(1)} %copy-done.3), kind=kOutput, calls=%fused_computation.10 | convolution fusion | flops 3482492928 | bytes 12312576 | tf_op jit(solution)/shard_map/rbp,kpq->krbq/dot_general | solution.py:84
  74.8 8.3 %copy.65 = bf16[16,276,8,128]{3,2,1,0:T(8,128)(2,1)} copy(bf16[16,276,8,128]{3,1,2,0:T(8,128)(2,1)} %convert_bitcast_fusion) | data formatting | bytes 18087936 | tf_op jit(solution)/shard_map/convert_element_type | solution.py:90
  83.1 14.0 %reshape.153 = bf16[16,276,1024]{2,1,0:T(8,128)(2,1)} reshape(bf16[16,276,8,128]{3,2,1,0:T(8,128)(2,1)} %copy.65) | data formatting | bytes 18087936 | tf_op jit(solution)/shard_map/convert_element_type | solution.py:90
  97.1 13.0 %fusion.6 = f32[256,1024]{1,0:T(8,128)S(1)} fusion(bf16[16,276,1024]{2,1,0:T(8,128)(2,1)} %reshape.153, bf16[1,16,256,1024]{3,2,1,0:T(8,128)(2,1)} %param.14, bf16[16,256,276]{1,0,2:T(8,128)(2,1)S(1)} %convert_bitcast_fusion.1), kind=kOutput, calls=%fused_computation.8 | convolution fusion | flops 2327576576 | bytes 20742144 | tf_op jit(solution)/shard_map/kyi,kix->kyx/dot_general | solution.py:94
  110.3 17.7 %fusion.45 = (bf16[16,276,1024]{2,1,0:T(8,128)(2,1)}, f32[16,276,1024]{2,1,0:T(8,128)}) fusion(bf16[1,16,256,1024]{3,2,1,0:T(8,128)(2,1)} %param.14, f32[256,1024]{1,0:T(8,128)S(1)} %bitcast.59, bf16[16,256,276]{1,0,2:T(8,128)(2,1)S(1)} %convert_bitcast_fusion.1), kind=kOutput, calls=%fused_computation.67 | convolution fusion | flops 2332360704 | bytes 38830080 | tf_op jit(solution)/shard_map/kyi,kyx->kix/dot_general | solution.py:100
  128.0 2.4 fusion.43
  130.3 1.9 collective-permute-start.2
  133.4 5.3 %collective-permute-start.3 = (bf16[16,10,1024]{2,1,0:T(8,128)(2,1)}, bf16[16,10,1024]{2,1,0:T(8,128)(2,1)}, u32[]{:S(2)}, u32[]{:S(2)}) collective-permute-start(bf16[16,10,1024]{2,1,0:T(8,128)(2,1)} %get-tuple-element.29), channel_id=1, source_target_pairs={{1,0},{2,1},{3,2},{5,4},{6,5},{7,6},{9,8},{10,9},{11,10},{13,12},{... | collective-permute-start | bytes 983048 | tf_op jit(solution)/shard_map/ppermute | solution.py:34
  140.6 12.6 %slice.108 = f32[16,256,1024]{2,1,0:T(8,128)} slice(f32[16,276,1024]{2,1,0:T(8,128)} %get-tuple-element.37), slice={[0:16], [10:266], [0:1024]} | slice | bytes 33554432 | tf_op jit(solution)/shard_map/slice | solution.py:105
  153.2 1.7 slice_add_fusion.1
  154.9 5.8 %scatter-add.6 = f32[16,256,1024]{2,1,0:T(8,128)} dynamic-update-slice(f32[16,256,1024]{2,1,0:T(8,128)} %slice.108, f32[16,10,1024]{2,1,0:T(8,128)S(1)} %slice_add_fusion.1, s32[]{:T(128)} %constant.75.clone.1, s32[]{:T(128)} %constant.75.clone.1, s32[]{:T(128)} %constant.75.clone.1) | dynamic-update-slice | bytes 1310724 | tf_op jit(solution)/shard_map/scatter-add | solution.py:106
  160.8 1.5 slice_add_fusion
  162.3 5.1 %scatter-add.9 = f32[16,256,1024]{2,1,0:T(8,128)} dynamic-update-slice(f32[16,256,1024]{2,1,0:T(8,128)} %scatter-add.6, f32[16,10,1024]{2,1,0:T(8,128)S(1)} %slice_add_fusion, s32[]{:T(128)} %constant.75.clone.1, s32[]{:T(128)} %constant.82.clone.1, s32[]{:T(128)} %constant.75.clone.1) | dynamic-update-slice | bytes 1310724 | tf_op jit(solution)/shard_map/scatter-add | solution.py:107
  167.4 9.1 %convert_element_type.94 = bf16[16,256,1024]{2,1,0:T(8,128)(2,1)} convert(f32[16,256,1024]{2,1,0:T(8,128)} %scatter-add.9) | non-fusion elementwise | flops 4194304 | bytes 25165824 | tf_op jit(solution)/shard_map/convert_element_type | solution.py:108
  176.5 12.3 %copy.73 = bf16[16,256,1024]{1,2,0:T(8,128)(2,1)} copy(bf16[16,256,1024]{2,1,0:T(8,128)(2,1)} %convert_element_type.94) | data formatting | bytes 16777216
  188.8 8.4 %pad.13.clone = bf16[16,256,1280]{1,2,0:T(8,128)(2,1)} pad(bf16[16,256,1024]{1,2,0:T(8,128)(2,1)} %copy.73, bf16[]{:T(256)} %constant.80.clone.1), padding=0_0x0_0x128_128 | pad | bytes 18874370 | tf_op jit(solution)/shard_map/jit(_pad)/pad | solution.py:64
  197.2 16.7 %fusion.42 = (bf16[16,256,8,128]{1,3,2,0:T(8,128)(2,1)}, bf16[16,256,8,128]{1,3,2,0:T(8,128)(2,1)}, bf16[16,256,8,128]{1,3,2,0:T(8,128)(2,1)}) fusion(bf16[16,256,10,128]{1,3,2,0:T(8,128)(2,1)} %bitcast.56), kind=kLoop, calls=%fused_computation.64 | loop fusion | bytes 50331648 | tf_op jit(solution)/shard_map/slice | solution.py:67
  213.9 11.4 %copy.70 = bf16[16,256,8,128]{3,1,0,2:T(8,128)(2,1)} copy(bf16[16,256,8,128]{1,3,2,0:T(8,128)(2,1)} %get-tuple-element.26) | data formatting | bytes 16777216
  225.3 11.4 %copy.71 = bf16[16,256,8,128]{3,1,0,2:T(8,128)(2,1)} copy(bf16[16,256,8,128]{1,3,2,0:T(8,128)(2,1)} %get-tuple-element.27) | data formatting | bytes 16777216
  236.7 11.4 %copy.72 = bf16[16,256,8,128]{3,1,0,2:T(8,128)(2,1)} copy(bf16[16,256,8,128]{1,3,2,0:T(8,128)(2,1)} %get-tuple-element.28) | data formatting | bytes 16777216
  248.1 12.3 %fusion = f32[256,8,128,1]{0,2,3,1:T(8,128)S(1)} fusion(bf16[16,256,8,128]{3,1,0,2:T(8,128)(2,1)} %copy.72, bf16[16,256,8,128]{3,1,0,2:T(8,128)(2,1)} %copy.71, bf16[16,256,8,128]{3,1,0,2:T(8,128)(2,1)} %copy.70, bf16[16,384,128]{1,2,0:T(8,128)(2,1)S(1)} %copy.60), kind=kOutput, calls=%fused_computation | convolution fusion | flops 3296722944 | bytes 27787264 | tf_op jit(solution)/shard_map/krbp,kpq->rbq/dot_general | solution.py:109
  260.4 2.4 broadcast_multiply_fusion
  262.8 169.3 %reduce-scatter.2.cloned.1.call-done = f32[4,256,32]{1,2,0:T(8,128)} async-done(((f32[4,256,1024]{1,2,0:T(8,128)}), f32[4,256,32]{1,2,0:T(8,128)}) %reduce-scatter.2.cloned.1.call-update) | async-done | bytes 131088 | tf_op jit(solution)/shard_map/reduce_scatter | solution.py:116
  (44 shorter events, 12.6 us)
Async XLA Ops:
  7.2 15.1 %copy-start = (bf16[16,21]{1,0:T(8,128)(2,1)S(1)}, bf16[16,21]{1,0:T(8,128)(2,1)}, u32[]{:S(2)}) copy-start(bf16[16,21]{1,0:T(8,128)(2,1)} %param.12) | copy-start | bytes 2020
  7.2 11.6 %copy-start.8 = (s32[32,1]{0,1:T(1,128)S(1)}, s32[32,1]{0,1:T(1,128)}, u32[]{:S(2)}) copy-start(s32[32,1]{0,1:T(1,128)} %param.16) | copy-start | bytes 388
  7.2 13.5 %copy-start.7 = (s32[1,256]{1,0:T(1,128)S(1)}, s32[1,256]{1,0:T(1,128)}, u32[]{:S(2)}) copy-start(s32[1,256]{1,0:T(1,128)} %param.17) | copy-start | bytes 3076
  7.2 17.4 %copy-start.6 = (bf16[16,21]{1,0:T(8,128)(2,1)S(1)}, bf16[16,21]{1,0:T(8,128)(2,1)}, u32[]{:S(2)}) copy-start(bf16[16,21]{1,0:T(8,128)(2,1)} %param.13) | copy-start | bytes 2020
  9.6 39.0 %all-to-all-start = ((bf16[32,4,256,32]{2,3,1,0:T(8,128)(2,1)}), bf16[32,4,256,32]{2,3,1,0:T(8,128)(2,1)}, u32[]{:S(2)}, u32[]{:S(2)}) async-start(bf16[32,4,256,32]{2,3,1,0:T(8,128)(2,1)} %stack.2), calls=%async_computation | async-start | bytes 4194304 | tf_op jit(solution)/shard_map/all_to_all | solution.py:10
  18.8 413.3 %reduce-scatter.2.cloned.1.call-start = ((), (), s32[]{:S(2)}) async-start(), calls=%async_computation.2 | async-start | bytes 4325376 | tf_op jit(solution)/shard_map/reduce_scatter | solution.py:116
  51.3 9.5 %collective-permute-start = (bf16[10,1024]{0,1:T(8,128)(2,1)}, bf16[10,1024]{0,1:T(8,128)(2,1)}, u32[]{:S(2)}, u32[]{:S(2)}) collective-permute-start(bf16[10,1024]{0,1:T(8,128)(2,1)} %get-tuple-element.31), channel_id=1, source_target_pairs={{0,1},{1,2},{2,3},{4,5},{5,6},{6,7},{8,9},{9,10},{10,11},{12,13},{... | collective-permute-start | bytes 61448 | tf_op jit(solution)/shard_map/ppermute | solution.py:22
  53.2 9.3 %collective-permute-start.1 = (bf16[10,1024]{0,1:T(8,128)(2,1)}, bf16[10,1024]{0,1:T(8,128)(2,1)}, u32[]{:S(2)}, u32[]{:S(2)}) collective-permute-start(bf16[10,1024]{0,1:T(8,128)(2,1)} %get-tuple-element.32), channel_id=1, source_target_pairs={{1,0},{2,1},{3,2},{5,4},{6,5},{7,6},{9,8},{10,9},{11,10},{13,12},{... | collective-permute-start | bytes 61448 | tf_op jit(solution)/shard_map/ppermute | solution.py:24
  66.2 1.4 copy-start.3
  97.1 13.0 %copy-start.5 = (bf16[1,256,1024]{2,1,0:T(8,128)(2,1)S(1)}, bf16[1,256,1024]{2,1,0:T(8,128)(2,1)}, u32[]{:S(2)}) copy-start(bf16[1,256,1024]{2,1,0:T(8,128)(2,1)} %param.15) | copy-start | bytes 1572868
  110.3 17.7 %copy-start.2 = (f32[1,256,1024]{2,1,0:T(8,128)}, f32[1,256,1024]{2,1,0:T(8,128)S(1)}, u32[]{:S(2)}) copy-start(f32[1,256,1024]{2,1,0:T(8,128)S(1)} %fusion.31) | copy-start | bytes 3145732
  110.3 22.0 %copy-start.4 = (s32[384,128]{1,0:T(8,128)S(1)}, s32[384,128]{1,0:T(8,128)}, u32[]{:S(2)}) copy-start(s32[384,128]{1,0:T(8,128)} %subtract_add_fusion) | copy-start | bytes 589828
  130.3 22.9 %collective-permute-start.2 = (bf16[16,10,1024]{2,1,0:T(8,128)(2,1)}, bf16[16,10,1024]{2,1,0:T(8,128)(2,1)}, u32[]{:S(2)}, u32[]{:S(2)}) collective-permute-start(bf16[16,10,1024]{2,1,0:T(8,128)(2,1)} %get-tuple-element.30), channel_id=1, source_target_pairs={{0,1},{1,2},{2,3},{4,5},{5,6},{6,7},{8,9},{9,10},{10,11},{12,13},{... | collective-permute-start | bytes 983048 | tf_op jit(solution)/shard_map/ppermute | solution.py:34
  133.4 27.4 %collective-permute-start.3 = (bf16[16,10,1024]{2,1,0:T(8,128)(2,1)}, bf16[16,10,1024]{2,1,0:T(8,128)(2,1)}, u32[]{:S(2)}, u32[]{:S(2)}) collective-permute-start(bf16[16,10,1024]{2,1,0:T(8,128)(2,1)} %get-tuple-element.29), channel_id=1, source_target_pairs={{1,0},{2,1},{3,2},{5,4},{6,5},{7,6},{9,8},{10,9},{11,10},{13,12},{... | collective-permute-start | bytes 983048 | tf_op jit(solution)/shard_map/ppermute | solution.py:34
  260.4 171.7 %copy-start.1 = (bf16[16,21]{1,0:T(8,128)(2,1)S(1)}, bf16[16,21]{1,0:T(8,128)(2,1)}, u32[]{:S(2)}) copy-start(bf16[16,21]{1,0:T(8,128)(2,1)} %param.12) | copy-start | bytes 2020
Sparse Core Ops, SparseCore 0:
  262.9 169.1 reduce-scatter.1
